TPU v7x, 512 devices: a whole 4x4x16 slice. The times are simulated.
512 devices in a mesh: cells: 64 (over z, x), snaps: 8 (over y, core).
Axes of the slice: x: 4, y: 4, z: 16, core: 2. Of those that a mesh axis runs over, the one named last changes fastest.
Arguments:
- snapshots: float32 [262144, 2048], P('cells', 'snaps'), may hold values from -6 to 6
- sketch: float32 [2048, 32], P('snaps'), may hold values from -6 to 6
Outputs:
- basis: float32 [32, 262144], P(None, 'cells')
- coefficients: float32 [32, 2048], P(None, 'snaps')
All inputs are finite; a program needn't handle non-finite values.
Results may differ from a plain program's by a relative error of at most 0.0003.
Values sent between devices are 32-bit elements; how exact they have to be, the bound alone decides.
A program may use at most 64 MiB of HBM per device.

v0:
```python
import math

import jax
import jax.numpy as jnp
from jax import lax
from jax.sharding import PartitionSpec as P


def partner_2(block, axis, distance):
    count = lax.axis_size(axis)
    route = []
    for low in range(count):
        high = low | 1 << distance
        if high != low and high < count:
            route += [(low, high), (high, low)]
    return lax.ppermute(block, axis, route)


def upper_factor(columns):
    count = columns.shape[0]
    places = jnp.arange(columns.shape[1])
    for step in range(count):
        column = columns[step]
        lower_part = jnp.where(places >= step, column, 0.0)
        length = jnp.sqrt(jnp.sum(lower_part * lower_part))
        sense = jnp.where(column[step] < 0, -1.0, 1.0)
        vector = lower_part + jnp.where(places == step, sense * length, 0.0)
        factor = 2.0 / jnp.sum(vector * vector)
        inner = jnp.dot(columns, vector, precision=lax.Precision.HIGHEST)
        columns = columns - factor * inner[:, None] * vector[None, :]
    upper = jnp.triu(columns[:, :count].T)
    diagonal = jnp.diagonal(upper)
    return jnp.where(diagonal[:, None] < 0, -upper, upper)


def lower_solve(lower_factor, rows):
    return lax.linalg.triangular_solve(lower_factor, rows, left_side=True, lower=True)


def upper_solve(upper, rows):
    return lower_solve(jnp.transpose(upper), rows)


def shards(snapshots, sketch):
    partial_rows = jnp.einsum("sk,ms->km", sketch, snapshots, precision=lax.Precision.HIGHEST)
    sketched = lax.psum(partial_rows, "snaps")
    total_cells = snapshots.shape[0] * lax.axis_size("cells")
    upper = upper_factor(sketched)
    position = lax.axis_index("cells")
    for bit in range(lax.axis_size("cells").bit_length() - 1):
        partner = partner_2(upper, "cells", bit)
        high_side = jnp.right_shift(position, bit) % 2 == 1
        first = jnp.where(high_side, partner, upper)
        second = jnp.where(high_side, upper, partner)
        upper = upper_factor(jnp.concatenate([first.T, second.T], axis=1))
    orth = upper_solve(upper, sketched)
    partial_coeffs = jnp.dot(orth, snapshots, precision=lax.Precision.HIGHEST)
    coefficients = lax.psum(partial_coeffs, "cells")
    basis = orth * math.sqrt(total_cells)
    return (basis, coefficients)


def solution(mesh):
    return jax.shard_map(
        shards,
        mesh=mesh,
        in_specs=(P("cells", "snaps"), P("snaps", None)),
        out_specs=(P(None, "cells"), P(None, "snaps")),
        check_vma=False,
    )
```

profile of v0, /device:TPU:8, one launch (start us, length us, event | category | flops | bytes accessed | tf_op | source)
XLA Modules:
  0.0 1405.5 jit_solution(5781502194587796289)
XLA Ops:
  7.9 6.8 fusion.519
  14.8 78.8 %all-reduce.2.cloned.1.call-done = f32[32,4096]{1,0:T(8,128)} async-done(((f32[32,4096]{1,0:T(8,128)}), f32[32,4096]{1,0:T(8,128)}) %all-reduce.2.cloned.1.call-update) | async-done | bytes 524304 | tf_op jit(solution)/shard_map/psum | solution.py:46
  95.9 1.2 slice.2293
  99.9 1.6 fusion.223
  101.5 1.2 multiply_subtract_fusion.30
  107.0 1.2 multiply_subtract_fusion.29
  207.1 1.2 multiply_subtract_fusion.9
  212.7 1.1 multiply_subtract_fusion.8
  218.3 1.1 multiply_subtract_fusion.7
  223.8 1.2 multiply_subtract_fusion.6
  229.4 1.3 multiply_subtract_fusion.5
  235.0 1.3 multiply_subtract_fusion.4
  240.7 1.4 multiply_subtract_fusion.3
  246.5 1.6 multiply_subtract_fusion.2
  252.5 1.5 multiply_subtract_fusion.1
  258.4 1.6 multiply_subtract_fusion
  265.3 3.4 collective-permute-start
  268.6 2.2 collective-permute-done
  403.5 5.3 collective-permute-start.1
  408.8 1.8 collective-permute-done.1
  543.2 3.6 collective-permute-start.2
  546.8 2.0 collective-permute-done.2
  681.4 4.7 collective-permute-start.3
  686.1 1.8 collective-permute-done.3
  820.5 7.9 collective-permute-start.4
  828.4 1.6 collective-permute-done.4
  962.7 13.1 collective-permute-start.5
  975.8 1.5 collective-permute-done.5
  1109.9 2.4 custom-call.3
  1112.4 1.4 broadcast_multiply_fusion
  1113.8 4.3 fusion.520
  1118.1 280.0 %psum.15 = f32[32,256]{1,0:T(8,128)} all-reduce(f32[32,256]{1,0:T(8,128)S(1)} %fusion.520), channel_id=1, replica_groups=mesh['cells'=64,'snaps'=8] {'cells'}, use_global_device_ids=true, to_apply=%region_449.450 | all-reduce | flops 8192 | bytes 65536 | tf_op jit(solution)/shard_map/psum | solution.py:58
  (1398 shorter events, 491.3 us)
Async XLA Ops:
  7.2 0.8 copy-start
  7.2 86.4 %all-reduce.2.cloned.1.call-start = ((), (), s32[]{:S(2)}) async-start(), calls=%async_computation | async-start | bytes 1048576 | tf_op jit(solution)/shard_map/psum | solution.py:46
  93.6 19.1 %copy-start.1 = (f32[32,4096]{1,0:T(8,128)S(1)}, f32[32,4096]{1,0:T(8,128)}, u32[]{:S(2)}) copy-start(f32[32,4096]{1,0:T(8,128)} %all-reduce.2.cloned.1.call-done) | copy-start | bytes 1572868
  265.3 5.6 collective-permute-start
  403.5 7.1 collective-permute-start.1
  543.2 5.6 collective-permute-start.2
  681.4 6.5 collective-permute-start.3
  820.5 9.5 collective-permute-start.4
  962.7 14.6 %collective-permute-start.5 = (f32[32,32]{0,1:T(8,128)S(1)}, f32[32,32]{0,1:T(8,128)S(1)}, u32[]{:S(2)}, u32[]{:S(2)}) collective-permute-start(f32[32,32]{0,1:T(8,128)S(1)} %negate_select_fusion.1), channel_id=1, source_target_pairs={{0,256},{256,0},{8,264},{264,8},{16,272},{272,16},{24,280},{280,24... | collective-permute-start | bytes 12296 | tf_op jit(solution)/shard_map/ppermute | solution.py:16
Sparse Core Ops, SparseCore 0:
  14.9 78.6 all-reduce.1
where the time goes:
time: 1420 us; the launch traced here: 1410 us
  between operations  473 us (33%)
  other arithmetic  330 us (23%)
  blocking collectives  280 us (20%)
  local copies, waits for them, and re-layouts  138 us (10%)
  waiting for transfers between devices  89.8 us (6%)
  matrix products  56.3 us (4%)
  starting transfers between devices  38 us (3%)
    psum x1, blocking collectives, shards(): coefficients = lax.psum(partial_coeffs, 'cells')  280 us
    reduce_sum x224, other arithmetic, upper_factor(): factor = 2.0 / jnp.sum(vector * vector)  135 us
    reduce_sum x224, other arithmetic, upper_factor(): length = jnp.sqrt(jnp.sum(lower_part * lower_part))  135 us
    slice x224, local copies, waits for them, and re-layouts, upper_factor(): sense = jnp.where(column[step] < 0, -1.0, 1.0)  131 us
    psum x1, waiting for transfers between devices, shards(): sketched = lax.psum(partial_rows, 'snaps')  78.8 us
    sub x217, other arithmetic, upper_factor(): columns = columns - factor * inner[:, None] * vector[None, :]  53.5 us
    dot_general x224, matrix products, upper_factor(): inner = jnp.dot(columns, vector, precision=lax.Precision.HIGHEST)  43.8 us
    ppermute x6, starting transfers between devices, partner_2(): return lax.ppermute(block, axis, route)  37.9 us
  transfers between devices with their start and end apart: 7, of which 7 were waited for; matrix products, arithmetic and copies ran while one was open for 0% of the time, Pallas kernels for 0%

commit v1 on v0

v1 whole, which is shorter than its diff:
```python
import functools
import math

import jax
import jax.numpy as jnp
from jax import lax
from jax.experimental import pallas as pl
from jax.experimental.pallas import tpu as pltpu
from jax.sharding import PartitionSpec as P

MESH = pl.DeviceIdType.MESH
NX = 4
F32 = jnp.float32
BF16 = jnp.bfloat16
ROWS = 32


def two_sum(a, b):
    s = a + b
    t = s - a
    return s, (a - (s - t)) + (b - t)


def quick_two_sum(a, b):
    s = a + b
    return s, b - (s - a)


def halves(a):
    c = a * 4097.0
    high = c - (c - a)
    return high, a - high


def two_prod(a, ah, al, b, bh, bl):
    p = a * b
    return p, ((ah * bh - p) + ah * bl + al * bh) + al * bl


def dd_add(ah, al, bh, bl):
    s, e = two_sum(ah, bh)
    return quick_two_sum(s, e + (al + bl))


def thirds(a):
    h = a.astype(BF16)
    rest = a - h.astype(F32)
    m = rest.astype(BF16)
    low = (rest - m.astype(F32)).astype(BF16)
    return h, m, low


def dot(a, b, transposed=False):
    dims = (((1,), (1 if transposed else 0,)), ((), ()))
    return lax.dot_general(a, b, dims, preferred_element_type=F32)


def six(lhs, h, m, low, transposed):
    n = ROWS
    dh = dot(lhs, h, transposed)
    dm = dot(lhs[: 2 * n], m, transposed)
    dl = dot(lhs[:n], low, transposed)
    small = (dh[2 * n :] + dm[n:]) + dl
    return dh[:n] + ((dh[n : 2 * n] + dm[:n]) + small)


def sum_pairs(pairs):
    while len(pairs) > 1:
        pairs = [
            dd_add(*pairs[i], *pairs[i + 1]) if i + 1 < len(pairs) else pairs[i]
            for i in range(0, len(pairs), 2)
        ]
    return pairs[0]


def power_above(x):
    p = jnp.full(x.shape, 2.0**-63, F32)
    inverse = jnp.full(x.shape, 2.0**63, F32)
    for step in (64, 32, 16, 8, 4, 2, 1):
        larger = x >= p * (2.0**step)
        p = jnp.where(larger, p * (2.0**step), p)
        inverse = jnp.where(larger, inverse * (2.0**-step), inverse)
    return p * 2.0, inverse * 0.5


def eliminate(gh, gl):
    gh, gl = list(gh), list(gl)
    tiles = len(gh)
    sub = lax.broadcasted_iota(jnp.int32, (8, 128), 0)
    lane = lax.broadcasted_iota(jnp.int32, (8, 128), 1)
    for k in range(8 * tiles - 1):
        ib, kr = divmod(k, 8)
        rh = jnp.broadcast_to(gh[ib][kr : kr + 1, :], (8, 128))
        rl = jnp.broadcast_to(gl[ib][kr : kr + 1, :], (8, 128))
        ph = jnp.broadcast_to(rh[:, k : k + 1], (8, 128))
        plo = jnp.broadcast_to(rl[:, k : k + 1], (8, 128))
        r = 1.0 / ph
        pa, pb = halves(ph)
        q1 = rh * r
        qa, qb = halves(q1)
        t, te = two_prod(q1, qa, qb, ph, pa, pb)
        rest = (rh - t) - te + (rl - q1 * plo)
        uh, ul = quick_two_sum(q1, rest * r)
        ua, ub = halves(uh)
        for t in range(ib if kr < 7 else ib + 1, tiles):
            ch = jnp.broadcast_to(gh[t][:, k : k + 1], (8, 128))
            cl = jnp.broadcast_to(gl[t][:, k : k + 1], (8, 128))
            if t == ib:
                ch = jnp.where(sub > kr, ch, 0.0)
                cl = jnp.where(sub > kr, cl, 0.0)
            ca, cb = halves(ch)
            p, pe = two_prod(ch, ca, cb, uh, ua, ub)
            pe = pe + (ch * ul + cl * uh)
            s, e = two_sum(gh[t], -p)
            gh[t], gl[t] = quick_two_sum(s, e + (gl[t] - pe))
    out = []
    for t in range(tiles):
        at = lane == sub + 8 * t
        d = jnp.sum(jnp.where(at, gh[t], 0.0), axis=1, keepdims=True)
        y = lax.rsqrt(d)
        y = y * (1.5 - 0.5 * d * y * y)
        out.append((gh[t] + gl[t]) * y)
    return out


def kernel(
    nz, ch, total_cells,
    a_ref, w_ref, basis_ref, coef_ref,
    a_buf, a_h, a_m, a_l,
    send_a, got_a, rs_a, rs_b, rs_c, rs_d, s_all, s_cat,
    x_bf, p_ref, sig, gx, gz, ga, gt,
    wp, wx, wz, wa,
    load_sem, s_a, r_a, s_b, r_b, s_y, r_y, s_f, r_f, s_p, r_p, s_m, r_m,
):
    cells = lax.axis_index("cells")
    snaps = lax.axis_index("snaps")
    z, x = cells // NX, cells % NX
    y, core = snaps // 2, snaps % 2
    n = ROWS
    up, down, far = (y + 1) % 4, (y + 3) % 4, (y + 2) % 4
    mate = (cells, y * 2 + (1 - core))
    above = (cells, up * 2 + core)
    below = (cells, down * 2 + core)
    snap_peers = [(cells, (snaps + d) % 8) for d in (4, 5, 3, 2, 6, 1, 7)]
    x_peers = [(z * NX + (x + d) % NX, snaps) for d in range(1, NX)]
    z_steps = sorted(range(1, nz), key=lambda d: -min(d, nz - d))
    z_peers = [(((z + d) % nz) * NX + x, snaps) for d in z_steps]

    def remote(src, dst, ss, rs, to):
        return pltpu.make_async_remote_copy(
            src_ref=src, dst_ref=dst, send_sem=ss, recv_sem=rs,
            device_id=to, device_id_type=MESH,
        )

    barrier = pltpu.get_barrier_semaphore()
    everyone = z_peers + x_peers + snap_peers
    for peer in everyone:
        pl.semaphore_signal(barrier, inc=1, device_id=peer, device_id_type=MESH)

    offsets = (far, up, down, y)
    order = [(1 - core, o) for o in offsets] + [(core, o) for o in offsets]
    chunk_of = [c * 4 + o for c, o in order]
    loads = []
    for i, q in enumerate(chunk_of):
        start = pl.multiple_of(q * ch, ch)
        loads.append(
            pltpu.make_async_copy(a_ref.at[pl.ds(start, ch), :], a_buf.at[i], load_sem.at[i])
        )
        loads[-1].start()

    w_h, w_m, w_l = thirds(w_ref[...])
    w_cat = jnp.concatenate([w_h, w_m, w_l], axis=0)

    def sketch_chunk(i):
        loads[i].wait()
        h, m, low = thirds(a_buf[i])
        a_h[i], a_m[i], a_l[i] = h, m, low
        return six(w_cat, h, m, low, True)

    swaps = []
    for i in range(4):
        send_a[i] = sketch_chunk(i)
        if i == 0:
            pl.semaphore_wait(barrier, len(everyone))
        swaps.append(remote(send_a.at[i], got_a.at[i], s_a.at[i], r_a.at[i], mate))
        swaps[-1].start()

    far_part = sketch_chunk(4)
    swaps[0].wait_recv()
    rs_a[...] = far_part + got_a[0]
    b_up = remote(rs_a.at[0:16], rs_b.at[0], s_b.at[0], r_b.at[0], above)
    b_up.start()
    b_down = remote(rs_a.at[16:32], rs_b.at[1], s_b.at[1], r_b.at[1], below)
    b_down.start()
    up_part = sketch_chunk(5)
    swaps[1].wait_recv()
    up_part = up_part + got_a[1]
    rs_c[0, 16:32] = up_part[16:32]
    down_part = sketch_chunk(6)
    swaps[2].wait_recv()
    down_part = down_part + got_a[2]
    rs_c[1, 0:16] = down_part[0:16]
    b_up.wait_recv()
    rs_c[0, 0:16] = up_part[0:16] + rs_b[0]
    c_up = remote(rs_c.at[0], rs_d.at[0], s_b.at[2], r_b.at[2], above)
    c_up.start()
    b_down.wait_recv()
    rs_c[1, 16:32] = down_part[16:32] + rs_b[1]
    c_down = remote(rs_c.at[1], rs_d.at[1], s_b.at[3], r_b.at[3], below)
    c_down.start()
    own_part = sketch_chunk(7)
    swaps[3].wait_recv()
    own_part = own_part + got_a[3]
    c_up.wait_recv()
    own_part = own_part + rs_d[0]
    c_down.wait_recv()
    own = core * 4 + y
    s_all[own] = own_part + rs_d[1]

    g_up = remote(s_all.at[own], s_all.at[own], s_y.at[0], r_y.at[0], above)
    g_up.start()
    g_down = remote(s_all.at[own], s_all.at[own], s_y.at[1], r_y.at[1], below)
    g_down.start()

    def pass_on(slot, sem):
        copy = remote(s_all.at[slot], s_all.at[slot], s_p.at[sem], r_p.at[sem], mate)
        copy.start()
        return copy

    passes = [pass_on(own, 0)]

    def projected(i, slot):
        s_h, s_m, s_l = thirds(s_all[slot])
        s_cat[slot, 0:n] = s_h
        s_cat[slot, n : 2 * n] = s_m
        s_cat[slot, 2 * n : 3 * n] = s_l
        s_cat[slot, 3 * n : 4 * n] = s_h
        s_cat[slot, 4 * n : 5 * n] = s_m
        s_cat[slot, 5 * n : 6 * n] = s_h
        lhs = jnp.concatenate([s_h, s_m, s_l], axis=0)
        return six(lhs, a_h[i], a_m[i], a_l[i], False)

    w_sum = projected(7, own)
    passes[0].wait_recv()
    w_sum += projected(3, (1 - core) * 4 + y)
    slot_down, slot_up, slot_far = core * 4 + down, core * 4 + up, core * 4 + far
    arrived = remote(s_all.at[slot_down], s_all.at[slot_down], s_y.at[0], r_y.at[0], above)
    arrived.wait_recv()
    f_up = remote(
        s_all.at[slot_down, 0:16], s_all.at[slot_down, 0:16], s_f.at[0], r_f.at[0], above
    )
    f_up.start()
    passes.append(pass_on(slot_down, 1))
    arrived = remote(s_all.at[slot_up], s_all.at[slot_up], s_y.at[1], r_y.at[1], below)
    arrived.wait_recv()
    f_down = remote(
        s_all.at[slot_up, 16:32], s_all.at[slot_up, 16:32], s_f.at[1], r_f.at[1], below
    )
    f_down.start()
    passes.append(pass_on(slot_up, 2))
    w_sum += projected(6, slot_down)
    w_sum += projected(5, slot_up)
    passes[1].wait_recv()
    w_sum += projected(2, (1 - core) * 4 + down)
    passes[2].wait_recv()
    w_sum += projected(1, (1 - core) * 4 + up)
    f_up.wait_recv()
    f_down.wait_recv()
    passes.append(pass_on(slot_far, 3))
    w_sum += projected(4, slot_far)
    passes[3].wait_recv()
    w_sum += projected(0, (1 - core) * 4 + far)

    share = n // NX
    for i in range(NX):
        wp[i] = w_sum[i * share : (i + 1) * share]
    wx[x] = wp[x]
    for peer in x_peers:
        remote(wp.at[peer[0] % NX], wx.at[x], s_m.at[0], r_m.at[0], peer).start()

    top = jnp.max(jnp.abs(s_all[0]), axis=1, keepdims=True)
    for q in range(1, 8):
        top = jnp.maximum(top, jnp.max(jnp.abs(s_all[q]), axis=1, keepdims=True))
    scale, inverse = power_above(jnp.broadcast_to(top, (n, 128)))
    sig[...] = scale
    up_scale = inverse[:, 0:1] * 64.0
    p_sum = None
    for q in range(8):
        v = s_all[q] * up_scale
        parts = []
        for a in range(4):
            whole = jnp.round(v)
            parts.append(whole.astype(BF16))
            v = (v - whole) * 128.0
        x_bf[...] = jnp.concatenate(parts, axis=0)
        term = dot(x_bf[...], x_bf[...], True)
        p_sum = term if p_sum is None else p_sum + term
    p_ref[...] = p_sum
    part = p_ref[pl.ds(snaps, 16, stride=8), :]
    lane = lax.broadcasted_iota(jnp.int32, (4, 128), 1)
    group = lane // n
    lane_weight = jnp.where(
        group == 0, 2.0**-12, jnp.where(group == 1, 2.0**-19, jnp.where(group == 2, 2.0**-26, 2.0**-33))
    )
    gh = part[0:4] * lane_weight
    gl = jnp.zeros((4, 128), F32)
    for a in range(1, 4):
        gh, gl = dd_add(gh, gl, part[4 * a : 4 * a + 4] * (lane_weight * 2.0 ** (-7 * a)), 0.0)
    for turn in (64, 32):
        gh, gl = dd_add(gh, gl, pltpu.roll(gh, turn, 1), pltpu.roll(gl, turn, 1))
    row_scale = sig[pl.ds(snaps, 4, stride=8), :]
    wide = lax.broadcasted_iota(jnp.int32, (n, 128), 1)
    tall = lax.broadcasted_iota(jnp.int32, (n, 128), 0)
    column_scale = jnp.sum(jnp.where(wide % n == tall, scale, 0.0), axis=0, keepdims=True)
    both = row_scale * column_scale
    pick = lax.broadcasted_iota(jnp.int32, (4, 128), 0) == group
    gx[x, 0] = jnp.sum(jnp.where(pick, gh * both, 0.0), axis=0, keepdims=True)
    gx[x, 1] = jnp.sum(jnp.where(pick, gl * both, 0.0), axis=0, keepdims=True)

    def slots(buf, count):
        return buf.at[pl.ds(0, count)]

    for peer in x_peers:
        remote(gx.at[x], gx.at[x], s_m.at[1], r_m.at[1], peer).start()
    few = remote(slots(gx, NX - 1), slots(gx, NX - 1), s_m.at[1], r_m.at[1], mate)
    few.wait_recv()
    hi, lo = sum_pairs([(gx[i, 0], gx[i, 1]) for i in range(NX)])
    gz[z, 0], gz[z, 1] = hi, lo
    for peer in z_peers:
        remote(gz.at[z], gz.at[z], s_m.at[2], r_m.at[2], peer).start()

    w_few = remote(slots(wx, NX - 1), slots(wx, NX - 1), s_m.at[0], r_m.at[0], mate)
    w_few.wait_recv()
    row_sum = wx[0]
    for i in range(1, NX):
        row_sum = row_sum + wx[i]
    wz[z] = row_sum
    for peer in z_peers:
        remote(wz.at[z], wz.at[z], s_m.at[3], r_m.at[3], peer).start()

    g_many = remote(slots(gz, nz - 1), slots(gz, nz - 1), s_m.at[2], r_m.at[2], mate)
    g_many.wait_recv()
    hi, lo = sum_pairs([(gz[i, 0], gz[i, 1]) for i in range(nz)])
    ga[snaps, 0], ga[snaps, 1] = hi, lo
    for peer in snap_peers:
        remote(ga.at[snaps], ga.at[snaps], s_m.at[4], r_m.at[4], peer).start()
    g_seven = remote(slots(ga, 7), slots(ga, 7), s_m.at[4], r_m.at[4], mate)
    g_seven.wait_recv()

    for r in range(8):
        gt[0, r : r + 1, :] = ga[r, 0]
        gt[1, r : r + 1, :] = ga[r, 1]
    lane8 = lax.broadcasted_iota(jnp.int32, (8, 128), 1)
    sub8 = lax.broadcasted_iota(jnp.int32, (8, 128), 0)
    tiles_h, tiles_l = [], []
    for i in range(4):
        eye = jnp.where(lane8 - n == sub8 + 8 * i, 1.0, 0.0)
        turned_h = gt[0] if i == 0 else pltpu.roll(gt[0], 128 - n * i, 1)
        turned_l = gt[1] if i == 0 else pltpu.roll(gt[1], 128 - n * i, 1)
        tiles_h.append(jnp.where(lane8 < n, turned_h, eye))
        tiles_l.append(jnp.where(lane8 < n, turned_l, 0.0))
    factor = jnp.concatenate(eliminate(tiles_h, tiles_l), axis=0)
    f_h, f_m, f_l = thirds(factor)
    f_h, f_m, f_l = f_h.astype(F32), f_m.astype(F32), f_l.astype(F32)
    which = wide // n
    first = jnp.where(
        which == 0, pltpu.roll(f_h, 96, 1),
        jnp.where(which == 1, f_h, jnp.where(which == 2, pltpu.roll(f_h, 32, 1), pltpu.roll(f_m, 64, 1))),
    )
    second = jnp.where(which == 0, pltpu.roll(f_m, 96, 1), f_l)
    inv_cat = jnp.concatenate([first, second[:, : 2 * n]], axis=1).astype(BF16)
    root = math.sqrt(total_cells)
    for q in range(8):
        basis_ref[:, q * ch : (q + 1) * ch] = dot(inv_cat, s_cat[q]) * root

    w_many = remote(slots(wz, nz - 1), slots(wz, nz - 1), s_m.at[3], r_m.at[3], mate)
    w_many.wait_recv()
    rows = [wz[i] for i in range(nz)]
    while len(rows) > 1:
        rows = [rows[i] + rows[i + 1] for i in range(0, len(rows), 2)]
    wa[x] = rows[0]
    for peer in x_peers:
        remote(wa.at[x], wa.at[x], s_m.at[5], r_m.at[5], peer).start()
    wa_few = remote(slots(wa, NX - 1), slots(wa, NX - 1), s_m.at[5], r_m.at[5], mate)
    wa_few.wait_recv()
    w_total = jnp.concatenate([wa[i] for i in range(NX)], axis=0)
    t_h, t_m, t_l = thirds(w_total)
    w_parts = jnp.concatenate([t_h, t_m, t_l, t_h, t_m, t_h], axis=0)
    coef_ref[...] = dot(inv_cat, w_parts)

    for copy in swaps + [b_up, b_down, c_up, c_down, g_up, g_down, f_up, f_down] + passes:
        copy.wait_send()
    for copy in (w_few, few, g_many, w_many, g_seven, wa_few):
        copy.wait_send()


def shards(snapshots, sketch):
    cells, snaps = snapshots.shape
    n = sketch.shape[1]
    nz = lax.axis_size("cells") // NX
    ch = cells // 8
    total = cells * lax.axis_size("cells")
    dma = pltpu.SemaphoreType.DMA
    vm = pltpu.VMEM
    return pl.pallas_call(
        functools.partial(kernel, nz, ch, total),
        out_shape=(
            jax.ShapeDtypeStruct((n, cells), F32),
            jax.ShapeDtypeStruct((n, snaps), F32),
        ),
        in_specs=[
            pl.BlockSpec(memory_space=pl.ANY),
            pl.BlockSpec(memory_space=pltpu.VMEM),
        ],
        out_specs=(
            pl.BlockSpec(memory_space=pltpu.VMEM),
            pl.BlockSpec(memory_space=pltpu.VMEM),
        ),
        scratch_shapes=[
            vm((8, ch, snaps), F32),
            vm((8, ch, snaps), BF16), vm((8, ch, snaps), BF16), vm((8, ch, snaps), BF16),
            vm((4, n, ch), F32), vm((4, n, ch), F32),
            vm((n, ch), F32), vm((2, n // 2, ch), F32),
            vm((2, n, ch), F32), vm((2, n, ch), F32),
            vm((8, n, ch), F32), vm((8, 6 * n, ch), BF16),
            vm((4 * n, ch), BF16), vm((128, 128), F32), vm((n, 128), F32),
            vm((NX, 2, 1, 128), F32), vm((nz, 2, 1, 128), F32),
            vm((8, 2, 1, 128), F32), vm((2, 8, 128), F32),
            vm((NX, n // NX, snaps), F32), vm((NX, n // NX, snaps), F32),
            vm((nz, n // NX, snaps), F32), vm((NX, n // NX, snaps), F32),
            dma((8,)), dma((4,)), dma((4,)), dma((4,)), dma((4,)),
            dma((2,)), dma((2,)), dma((2,)), dma((2,)), dma((4,)), dma((4,)),
            dma((6,)), dma((6,)),
        ],
        compiler_params=pltpu.CompilerParams(collective_id=0, has_side_effects=True),
    )(snapshots, jnp.transpose(sketch))


def solution(mesh):
    return jax.shard_map(
        shards,
        mesh=mesh,
        in_specs=(P("cells", "snaps"), P("snaps", None)),
        out_specs=(P(None, "cells"), P(None, "snaps")),
        check_vma=False,
    )
```

time: 1420 us -> 62 us (0.04)
  the two profiles are of different devices: /device:TPU:8 before, /device:TPU:1 now
where the time goes in v1:
time: 62 us; the launch traced here: 61.7 us
  Pallas kernels  57.9 us (93%)
  local copies, waits for them, and re-layouts  3.24 us (5%)
  between operations  0.64 us (1%)
    pallas_call x1, Pallas kernels, shards(): pl.pallas_call(functools.partial(kernel, nz, ch, total), out_shape=(jax.S...  57.9 us
    unnamed x2, local copies, waits for them, and re-layouts  3.24 us

profile of v1, /device:TPU:1, one launch (start us, length us, event | category | flops | bytes accessed | tf_op | source)
XLA Modules:
  0.0 61.7 jit_solution(7446529578785136296)
XLA Ops:
  0.6 57.9 %shard_map.41 = (f32[32,4096]{1,0:T(8,128)}, f32[32,256]{1,0:T(8,128)}) custom-call(f32[4096,256]{1,0:T(8,128)} %a_ref.1, f32[32,256]{1,0:T(8,128)} %bitcast.1), custom_call_target="tpu_custom_call" | custom-call | tf_op jit(solution)/shard_map/pallas_call | solution.py:405
  58.5 1.9 %copy.6 = f32[32,4096]{1,0:T(8,128)} copy(f32[32,4096]{1,0:T(8,128)} %get-tuple-element.4) | data formatting | bytes 1048576
  60.4 1.4 %copy.7 = f32[32,256]{1,0:T(8,128)} copy(f32[32,256]{1,0:T(8,128)} %get-tuple-element.5) | data formatting | bytes 65536

commit v2 on v1

v2 whole, which is shorter than its diff:
```python
import functools
import math

import jax
import jax.numpy as jnp
from jax import lax
from jax.experimental import pallas as pl
from jax.experimental.pallas import tpu as pltpu
from jax.sharding import PartitionSpec as P

MESH = pl.DeviceIdType.MESH
NX = 4
F32 = jnp.float32
BF16 = jnp.bfloat16
ROWS = 32


def two_sum(a, b):
    s = a + b
    t = s - a
    return s, (a - (s - t)) + (b - t)


def quick_two_sum(a, b):
    s = a + b
    return s, b - (s - a)


def halves(a):
    c = a * 4097.0
    high = c - (c - a)
    return high, a - high


def two_prod(a, ah, al, b, bh, bl):
    p = a * b
    return p, ((ah * bh - p) + ah * bl + al * bh) + al * bl


def dd_add(ah, al, bh, bl):
    s, e = two_sum(ah, bh)
    return quick_two_sum(s, e + (al + bl))


def thirds(a):
    h = a.astype(BF16)
    rest = a - h.astype(F32)
    m = rest.astype(BF16)
    low = (rest - m.astype(F32)).astype(BF16)
    return h, m, low


def dot(a, b, transposed=False):
    dims = (((1,), (1 if transposed else 0,)), ((), ()))
    return lax.dot_general(a, b, dims, preferred_element_type=F32)


def six(lhs, h, m, low, transposed):
    n = ROWS
    dh = dot(lhs, h, transposed)
    dm = dot(lhs[: 2 * n], m, transposed)
    dl = dot(lhs[:n], low, transposed)
    small = (dh[2 * n :] + dm[n:]) + dl
    return dh[:n] + ((dh[n : 2 * n] + dm[:n]) + small)


def sum_pairs(pairs):
    while len(pairs) > 1:
        pairs = [
            dd_add(*pairs[i], *pairs[i + 1]) if i + 1 < len(pairs) else pairs[i]
            for i in range(0, len(pairs), 2)
        ]
    return pairs[0]


def power_above(x):
    p = jnp.full(x.shape, 2.0**-63, F32)
    inverse = jnp.full(x.shape, 2.0**63, F32)
    for step in (64, 32, 16, 8, 4, 2, 1):
        larger = x >= p * (2.0**step)
        p = jnp.where(larger, p * (2.0**step), p)
        inverse = jnp.where(larger, inverse * (2.0**-step), inverse)
    return p * 2.0, inverse * 0.5


def eliminate(gh, gl):
    gh, gl = list(gh), list(gl)
    tiles = len(gh)
    sub = lax.broadcasted_iota(jnp.int32, (8, 128), 0)
    lane = lax.broadcasted_iota(jnp.int32, (8, 128), 1)
    for k in range(8 * tiles - 1):
        ib, kr = divmod(k, 8)
        rh = jnp.broadcast_to(gh[ib][kr : kr + 1, :], (8, 128))
        rl = jnp.broadcast_to(gl[ib][kr : kr + 1, :], (8, 128))
        ph = jnp.broadcast_to(rh[:, k : k + 1], (8, 128))
        plo = jnp.broadcast_to(rl[:, k : k + 1], (8, 128))
        r = 1.0 / ph
        pa, pb = halves(ph)
        q1 = rh * r
        qa, qb = halves(q1)
        t, te = two_prod(q1, qa, qb, ph, pa, pb)
        rest = (rh - t) - te + (rl - q1 * plo)
        uh, ul = quick_two_sum(q1, rest * r)
        ua, ub = halves(uh)
        for t in range(ib if kr < 7 else ib + 1, tiles):
            ch = jnp.broadcast_to(gh[t][:, k : k + 1], (8, 128))
            cl = jnp.broadcast_to(gl[t][:, k : k + 1], (8, 128))
            if t == ib:
                ch = jnp.where(sub > kr, ch, 0.0)
                cl = jnp.where(sub > kr, cl, 0.0)
            ca, cb = halves(ch)
            p, pe = two_prod(ch, ca, cb, uh, ua, ub)
            pe = pe + (ch * ul + cl * uh)
            s, e = two_sum(gh[t], -p)
            gh[t], gl[t] = quick_two_sum(s, e + (gl[t] - pe))
    out = []
    for t in range(tiles):
        at = lane == sub + 8 * t
        d = jnp.sum(jnp.where(at, gh[t], 0.0), axis=1, keepdims=True)
        y = lax.rsqrt(d)
        y = y * (1.5 - 0.5 * d * y * y)
        out.append((gh[t] + gl[t]) * y)
    return out


def packed_gram(rows):
    n = ROWS
    top = jnp.max(jnp.abs(rows), axis=1, keepdims=True)
    scale, inverse = power_above(jnp.broadcast_to(top, (n, 128)))
    v = rows * (inverse[:, 0:1] * 64.0)
    parts = []
    for a in range(4):
        whole = jnp.round(v)
        parts.append(whole.astype(BF16))
        v = (v - whole) * 128.0
    slices = jnp.concatenate(parts, axis=0)
    products = dot(slices, slices, True)
    wide = lax.broadcasted_iota(jnp.int32, (n, 128), 1)
    tall = lax.broadcasted_iota(jnp.int32, (n, 128), 0)
    group = wide // n
    weight = jnp.where(
        group == 0, 2.0**-12,
        jnp.where(group == 1, 2.0**-19, jnp.where(group == 2, 2.0**-26, 2.0**-33)),
    )
    gh, gl = two_sum(products[0:n] * weight, products[n : 2 * n] * (weight * 2.0**-7))
    for a in (2, 3):
        gh, gl = dd_add(gh, gl, products[a * n : (a + 1) * n] * (weight * 2.0 ** (-7 * a)), 0.0)
    for turn in (64, 32):
        gh, gl = dd_add(gh, gl, pltpu.roll(gh, turn, 1), pltpu.roll(gl, turn, 1))
    column_scale = jnp.sum(jnp.where(wide - n * group == tall, scale, 0.0), axis=0, keepdims=True)
    both = scale * column_scale
    gh, gl = gh * both, gl * both
    lanes = lax.broadcasted_iota(jnp.int32, (8, 128), 1) // n

    def pack(g):
        out = g[0:8]
        for i in range(1, 4):
            out = jnp.where(lanes == i, g[8 * i : 8 * i + 8], out)
        return out

    return pack(gh), pack(gl)


def kernel(
    nz, ch, total_cells,
    a_ref, w_ref, basis_ref, coef_ref,
    a_buf, a_h, a_m, a_l,
    send_a, got_a, rs_a, rs_b, rs_c, rs_d, s_all, s_cat,
    go, gs, gx, gz, ga, gt,
    wp, wx, wz, wa, out_b, out_c,
    load_sem, s_a, r_a, s_b, r_b, s_c, r_c, s_y, r_y, s_f, r_f, s_p, r_p, s_m, r_m,
    out_sem, know_sem,
):
    cells = lax.axis_index("cells")
    snaps = lax.axis_index("snaps")
    n = ROWS
    ng, nu = 2 * NX, nz // 2
    z, x = lax.div(cells, NX), lax.rem(cells, NX)
    u, odd = lax.div(z, 2), lax.rem(z, 2)
    y, core = lax.div(snaps, 2), lax.rem(snaps, 2)
    g = 2 * x + odd
    up, down, far = lax.rem(y + 1, 4), lax.rem(y + 3, 4), lax.rem(y + 2, 4)
    mate = (cells, 2 * y + 1 - core)
    above = (cells, 2 * up + core)
    below = (cells, 2 * down + core)
    snap_of = [lax.rem(snaps + d, 8) for d in (4, 5, 3, 2, 6, 1, 7)]
    snap_peers = [(cells, s) for s in snap_of]
    g_of = [lax.rem(g + d, ng) for d in range(1, ng)]
    g_peers = [((2 * u + lax.rem(o, 2)) * NX + lax.div(o, 2), snaps) for o in g_of]

    def at_u(d):
        return ((2 * lax.rem(u + d, nu) + odd) * NX + x, snaps)

    u_peers = [at_u(d) for d in sorted(range(1, nu), key=lambda d: -min(d, nu - d))]

    def remote(src, dst, ss, rs, to):
        return pltpu.make_async_remote_copy(
            src_ref=src, dst_ref=dst, send_sem=ss, recv_sem=rs,
            device_id=to, device_id_type=MESH,
        )

    def signal(sem, to):
        pl.semaphore_signal(sem, inc=1, device_id=to, device_id_type=MESH)

    chunk_of = []
    for o in (far, up, down, y):
        chunk_of += [(1 - core) * 4 + o, core * 4 + o]
    loads = []
    for i, q in enumerate(chunk_of):
        start = pl.multiple_of(q * ch, ch)
        loads.append(
            pltpu.make_async_copy(a_ref.at[pl.ds(start, ch), :], a_buf.at[i], load_sem.at[i])
        )
        loads[-1].start()

    barrier = pltpu.get_barrier_semaphore()
    near = [at_u(1), at_u(nu - 1)] + g_peers + snap_peers
    for peer in near:
        signal(barrier, peer)

    w_h, w_m, w_l = thirds(w_ref[...])
    w_cat = jnp.concatenate([w_h, w_m, w_l], axis=0)

    def sketch_chunk(i):
        loads[i].wait()
        h, m, low = thirds(a_buf[i])
        a_h[i], a_m[i], a_l[i] = h, m, low
        return six(w_cat, h, m, low, True)

    swaps = []

    def swap(j):
        send_a[j] = sketch_chunk(2 * j)
        if j == 0:
            pl.semaphore_wait(barrier, len(near))
        swaps.append(remote(send_a.at[j], got_a.at[j], s_a.at[j], r_a.at[j], mate))
        swaps[-1].start()

    known = [1]

    def learn(part):
        while known[0] < nu // 2:
            d = known[0]
            sem = know_sem.at[d.bit_length() - 1]
            if part == 0:
                signal(sem, at_u(d))
                signal(sem, at_u(nu - d))
                return
            pl.semaphore_wait(sem, 2)
            known[0] = 2 * d
            return

    swap(0)
    learn(0)
    far_part = sketch_chunk(1)
    swap(1)
    up_part = sketch_chunk(3)
    swap(2)
    swaps[0].wait_recv()
    rs_a[...] = far_part + got_a[0]
    b_up = remote(rs_a.at[0:16], rs_b.at[0], s_b.at[0], r_b.at[0], above)
    b_up.start()
    b_down = remote(rs_a.at[16:32], rs_b.at[1], s_b.at[1], r_b.at[1], below)
    b_down.start()
    learn(1)
    learn(0)
    down_part = sketch_chunk(5)
    swaps[1].wait_recv()
    up_part = up_part + got_a[1]
    rs_c[0, 16:32] = up_part[16:32]
    c_up = [remote(rs_c.at[0, 16:32], rs_d.at[0, 16:32], s_c.at[0], r_c.at[0], above)]
    c_up[0].start()
    swap(3)
    swaps[2].wait_recv()
    down_part = down_part + got_a[2]
    rs_c[1, 0:16] = down_part[0:16]
    c_down = [remote(rs_c.at[1, 0:16], rs_d.at[1, 0:16], s_c.at[1], r_c.at[1], below)]
    c_down[0].start()
    own_part = sketch_chunk(7)
    b_up.wait_recv()
    rs_c[0, 0:16] = up_part[0:16] + rs_b[0]
    c_up.append(remote(rs_c.at[0, 0:16], rs_d.at[0, 0:16], s_c.at[2], r_c.at[2], above))
    c_up[1].start()
    b_down.wait_recv()
    rs_c[1, 16:32] = down_part[16:32] + rs_b[1]
    c_down.append(remote(rs_c.at[1, 16:32], rs_d.at[1, 16:32], s_c.at[3], r_c.at[3], below))
    c_down[1].start()
    swaps[3].wait_recv()
    own_part = own_part + got_a[3]
    learn(1)
    for copy in c_up + c_down:
        copy.wait_recv()
    own = core * 4 + y
    own_rows = own_part + rs_d[0] + rs_d[1]
    s_all[own] = own_rows

    first, second = pl.ds(0, 16), pl.ds(16, 16)

    def along(slot, rows, sem, to, s, r):
        piece = s_all.at[slot, rows]
        return remote(piece, piece, s.at[sem], r.at[sem], to)

    gathers = [
        along(own, first, 0, above, s_y, r_y),
        along(own, second, 1, below, s_y, r_y),
        along(own, second, 2, above, s_y, r_y),
        along(own, first, 3, below, s_y, r_y),
    ]
    for copy in gathers:
        copy.start()

    passes = []

    def pass_on(slot):
        sem = len(passes)
        copy = remote(s_all.at[slot], s_all.at[slot], s_p.at[sem], r_p.at[sem], mate)
        copy.start()
        passes.append(copy)

    pass_on(own)

    gram_h, gram_l = packed_gram(own_rows)
    for r in range(8):
        go[r, 0] = gram_h[r : r + 1]
        go[r, 1] = gram_l[r : r + 1]
    gs[snaps] = go[snaps]
    for s, peer in zip(snap_of, snap_peers):
        remote(go.at[s], gs.at[snaps], s_m.at[0], r_m.at[0], peer).start()

    def whole(buf, count, sem):
        piece = buf.at[pl.ds(0, count)]
        return remote(piece, piece, s_m.at[sem], r_m.at[sem], mate)

    def pair_sum(buf, count):
        return sum_pairs([(buf[i, 0], buf[i, 1]) for i in range(count)])

    def row_sum(buf, count):
        rows = [buf[i] for i in range(count)]
        while len(rows) > 1:
            rows = [rows[i] + rows[i + 1] for i in range(0, len(rows), 2)]
        return rows[0]

    def projected(i, slot):
        s_h, s_m, s_l = thirds(s_all[slot])
        s_cat[slot, 0:n] = s_h
        s_cat[slot, n : 2 * n] = s_m
        s_cat[slot, 2 * n : 3 * n] = s_l
        s_cat[slot, 3 * n : 4 * n] = s_h
        s_cat[slot, 4 * n : 5 * n] = s_m
        s_cat[slot, 5 * n : 6 * n] = s_h
        lhs = jnp.concatenate([s_h, s_m, s_l], axis=0)
        return six(lhs, a_h[i], a_m[i], a_l[i], False)

    theirs = (1 - core) * 4
    slot_down, slot_up, slot_far = core * 4 + down, core * 4 + up, core * 4 + far
    w_sum = projected(7, own)
    passes[0].wait_recv()
    w_sum += projected(6, theirs + y)
    along(slot_down, first, 0, above, s_y, r_y).wait_recv()
    f_up = along(slot_down, first, 0, above, s_f, r_f)
    f_up.start()
    along(slot_up, second, 1, below, s_y, r_y).wait_recv()
    f_down = along(slot_up, second, 1, below, s_f, r_f)
    f_down.start()
    along(slot_down, second, 2, above, s_y, r_y).wait_recv()
    pass_on(slot_down)
    along(slot_up, first, 3, below, s_y, r_y).wait_recv()
    pass_on(slot_up)

    gs_done = whole(gs, 7, 0)
    gs_done.wait_recv()
    hi, lo = pair_sum(gs, 8)
    gx[g, 0], gx[g, 1] = hi, lo
    for peer in g_peers:
        remote(gx.at[g], gx.at[g], s_m.at[1], r_m.at[1], peer).start()

    w_sum += projected(5, slot_down)
    w_sum += projected(3, slot_up)
    f_up.wait_recv()
    f_down.wait_recv()
    pass_on(slot_far)
    passes[1].wait_recv()
    w_sum += projected(4, theirs + down)
    passes[2].wait_recv()
    w_sum += projected(2, theirs + up)
    w_sum += projected(1, slot_far)
    passes[3].wait_recv()
    w_sum += projected(0, theirs + far)

    share = n // ng
    for i in range(ng):
        wp[i] = w_sum[i * share : (i + 1) * share]
    wx[g] = wp[g]
    for o, peer in zip(g_of, g_peers):
        remote(wp.at[o], wx.at[g], s_m.at[2], r_m.at[2], peer).start()

    gx_done = whole(gx, ng - 1, 1)
    gx_done.wait_recv()
    hi, lo = pair_sum(gx, ng)
    gz[u, 0], gz[u, 1] = hi, lo
    for peer in u_peers:
        remote(gz.at[u], gz.at[u], s_m.at[3], r_m.at[3], peer).start()

    wx_done = whole(wx, ng - 1, 2)
    wx_done.wait_recv()
    wz[u] = row_sum(wx, ng)
    for peer in u_peers:
        remote(wz.at[u], wz.at[u], s_m.at[4], r_m.at[4], peer).start()

    gz_done = whole(gz, nu - 1, 3)
    gz_done.wait_recv()
    hi, lo = pair_sum(gz, nu)
    ga[snaps, 0], ga[snaps, 1] = hi, lo
    for peer in snap_peers:
        remote(ga.at[snaps], ga.at[snaps], s_m.at[5], r_m.at[5], peer).start()
    ga_done = whole(ga, 7, 5)
    ga_done.wait_recv()

    for r in range(8):
        gt[0, r : r + 1, :] = ga[r, 0]
        gt[1, r : r + 1, :] = ga[r, 1]
    lane8 = lax.broadcasted_iota(jnp.int32, (8, 128), 1)
    sub8 = lax.broadcasted_iota(jnp.int32, (8, 128), 0)
    tiles_h, tiles_l = [], []
    for i in range(4):
        eye = jnp.where(lane8 - n == sub8 + 8 * i, 1.0, 0.0)
        turned_h = gt[0] if i == 0 else pltpu.roll(gt[0], 128 - n * i, 1)
        turned_l = gt[1] if i == 0 else pltpu.roll(gt[1], 128 - n * i, 1)
        tiles_h.append(jnp.where(lane8 < n, turned_h, eye))
        tiles_l.append(jnp.where(lane8 < n, turned_l, 0.0))
    factor = jnp.concatenate(eliminate(tiles_h, tiles_l), axis=0)

    wz_done = whole(wz, nu - 1, 4)
    wz_done.wait_recv()
    wa[g] = row_sum(wz, nu)
    for peer in g_peers:
        remote(wa.at[g], wa.at[g], s_m.at[6], r_m.at[6], peer).start()

    f_h, f_m, f_l = thirds(factor)
    f_h, f_m, f_l = f_h.astype(F32), f_m.astype(F32), f_l.astype(F32)
    which = lax.broadcasted_iota(jnp.int32, (n, 128), 1) // n
    left = jnp.where(
        which == 0, pltpu.roll(f_h, 96, 1),
        jnp.where(which == 1, f_h, jnp.where(which == 2, pltpu.roll(f_h, 32, 1), pltpu.roll(f_m, 64, 1))),
    )
    right = jnp.where(which == 0, pltpu.roll(f_m, 96, 1), f_l)
    inv_cat = jnp.concatenate([left, right[:, : 2 * n]], axis=1).astype(BF16)
    root = math.sqrt(total_cells)
    writes = []
    for q in range(8):
        columns = slice(q * ch, (q + 1) * ch)
        out_b[:, columns] = dot(inv_cat, s_cat[q]) * root
        writes.append(
            pltpu.make_async_copy(out_b.at[:, columns], basis_ref.at[:, columns], out_sem.at[q])
        )
        writes[-1].start()

    wa_done = whole(wa, ng - 1, 6)
    wa_done.wait_recv()
    w_total = jnp.concatenate([wa[i] for i in range(ng)], axis=0)
    t_h, t_m, t_l = thirds(w_total)
    out_c[...] = dot(inv_cat, jnp.concatenate([t_h, t_m, t_l, t_h, t_m, t_h], axis=0))
    writes.append(pltpu.make_async_copy(out_c, coef_ref, out_sem.at[8]))
    writes[-1].start()

    for copy in swaps + [b_up, b_down] + c_up + c_down + gathers + [f_up, f_down] + passes:
        copy.wait_send()
    for copy in (gs_done, gx_done, wx_done, gz_done, wz_done, ga_done, wa_done):
        copy.wait_send()
    for copy in writes:
        copy.wait()


def shards(snapshots, sketch):
    cells, snaps = snapshots.shape
    n = sketch.shape[1]
    nz = lax.axis_size("cells") // NX
    ch = cells // 8
    total = cells * lax.axis_size("cells")
    share = n // (2 * NX)
    dma = pltpu.SemaphoreType.DMA
    vm = pltpu.VMEM
    return pl.pallas_call(
        functools.partial(kernel, nz, ch, total),
        out_shape=(
            jax.ShapeDtypeStruct((n, cells), F32),
            jax.ShapeDtypeStruct((n, snaps), F32),
        ),
        in_specs=[
            pl.BlockSpec(memory_space=pl.ANY),
            pl.BlockSpec(memory_space=pltpu.VMEM),
        ],
        out_specs=(
            pl.BlockSpec(memory_space=pl.ANY),
            pl.BlockSpec(memory_space=pl.ANY),
        ),
        scratch_shapes=[
            vm((8, ch, snaps), F32),
            vm((8, ch, snaps), BF16), vm((8, ch, snaps), BF16), vm((8, ch, snaps), BF16),
            vm((4, n, ch), F32), vm((4, n, ch), F32),
            vm((n, ch), F32), vm((2, n // 2, ch), F32),
            vm((2, n, ch), F32), vm((2, n, ch), F32),
            vm((8, n, ch), F32), vm((8, 6 * n, ch), BF16),
            vm((8, 2, 1, 128), F32), vm((8, 2, 1, 128), F32),
            vm((2 * NX, 2, 1, 128), F32), vm((nz // 2, 2, 1, 128), F32),
            vm((8, 2, 1, 128), F32), vm((2, 8, 128), F32),
            vm((2 * NX, share, snaps), F32), vm((2 * NX, share, snaps), F32),
            vm((nz // 2, share, snaps), F32), vm((2 * NX, share, snaps), F32),
            vm((n, cells), F32), vm((n, snaps), F32),
            dma((8,)), dma((4,)), dma((4,)), dma((2,)), dma((2,)), dma((4,)), dma((4,)),
            dma((4,)), dma((4,)), dma((2,)), dma((2,)), dma((4,)), dma((4,)),
            dma((7,)), dma((7,)), dma((9,)), pltpu.SemaphoreType.REGULAR((2,)),
        ],
        compiler_params=pltpu.CompilerParams(collective_id=0, has_side_effects=True),
    )(snapshots, jnp.transpose(sketch))


def solution(mesh):
    return jax.shard_map(
        shards,
        mesh=mesh,
        in_specs=(P("cells", "snaps"), P("snaps", None)),
        out_specs=(P(None, "cells"), P(None, "snaps")),
        check_vma=False,
    )
```

time: 62 us -> 56.4 us (0.910)
  Pallas kernels: 57.9 us -> 52.2 us
    pallas_call x1, Pallas kernels: 57.9 us -> 52.2 us  [shards(): pl.pallas_call(functools.partial(kernel, nz, ch, total), out_shape=(jax.S...]
where the time goes in v2:
time: 56.4 us; the launch traced here: 56.1 us
  Pallas kernels  52.2 us (93%)
  local copies, waits for them, and re-layouts  3.24 us (6%)
  between operations  0.64 us (1%)
    pallas_call x1, Pallas kernels, shards(): pl.pallas_call(functools.partial(kernel, nz, ch, total), out_shape=(jax.S...  52.2 us
    unnamed x2, local copies, waits for them, and re-layouts  3.24 us

profile of v2, /device:TPU:1, one launch (start us, length us, event | category | flops | bytes accessed | tf_op | source)
XLA Modules:
  0.0 56.1 jit_solution(6558572202560305416)
XLA Ops:
  0.6 52.2 %shard_map.41 = (f32[32,4096]{1,0:T(8,128)}, f32[32,256]{1,0:T(8,128)}) custom-call(f32[4096,256]{1,0:T(8,128)} %a_ref.1, f32[32,256]{1,0:T(8,128)} %bitcast.1), custom_call_target="tpu_custom_call" | custom-call | tf_op jit(solution)/shard_map/pallas_call | solution.py:483
  52.9 1.9 %copy.6 = f32[32,4096]{1,0:T(8,128)} copy(f32[32,4096]{1,0:T(8,128)} %get-tuple-element.4) | data formatting | bytes 1048576
  54.7 1.4 %copy.7 = f32[32,256]{1,0:T(8,128)} copy(f32[32,256]{1,0:T(8,128)} %get-tuple-element.5) | data formatting | bytes 65536

commit v3 on v2

--- a/solution.py
+++ b/solution.py
@@ -83,17 +83,25 @@
     return p * 2.0, inverse * 0.5
 
 
-def eliminate(gh, gl):
+def eliminate(gh, gl, midway=None):
     gh, gl = list(gh), list(gl)
     tiles = len(gh)
     sub = lax.broadcasted_iota(jnp.int32, (8, 128), 0)
     lane = lax.broadcasted_iota(jnp.int32, (8, 128), 1)
+
+    def across(tile, k):
+        return jnp.broadcast_to(tile[:, k : k + 1], (8, 128))
+
+    def down(tile, r):
+        return jnp.broadcast_to(tile[r : r + 1, :], (8, 128))
+
     for k in range(8 * tiles - 1):
+        if midway is not None and k == 24:
+            midway()
         ib, kr = divmod(k, 8)
-        rh = jnp.broadcast_to(gh[ib][kr : kr + 1, :], (8, 128))
-        rl = jnp.broadcast_to(gl[ib][kr : kr + 1, :], (8, 128))
-        ph = jnp.broadcast_to(rh[:, k : k + 1], (8, 128))
-        plo = jnp.broadcast_to(rl[:, k : k + 1], (8, 128))
+        columns = {t: (across(gh[t], k), across(gl[t], k)) for t in range(ib, tiles)}
+        ph, plo = down(columns[ib][0], kr), down(columns[ib][1], kr)
+        rh, rl = down(gh[ib], kr), down(gl[ib], kr)
         r = 1.0 / ph
         pa, pb = halves(ph)
         q1 = rh * r
@@ -103,8 +111,7 @@
         uh, ul = quick_two_sum(q1, rest * r)
         ua, ub = halves(uh)
         for t in range(ib if kr < 7 else ib + 1, tiles):
-            ch = jnp.broadcast_to(gh[t][:, k : k + 1], (8, 128))
-            cl = jnp.broadcast_to(gl[t][:, k : k + 1], (8, 128))
+            ch, cl = columns[t]
             if t == ib:
                 ch = jnp.where(sub > kr, ch, 0.0)
                 cl = jnp.where(sub > kr, cl, 0.0)
@@ -164,7 +171,7 @@
 def kernel(
     nz, ch, total_cells,
     a_ref, w_ref, basis_ref, coef_ref,
-    a_buf, a_h, a_m, a_l,
+    w_buf, a_buf, a_h, a_m, a_l,
     send_a, got_a, rs_a, rs_b, rs_c, rs_d, s_all, s_cat,
     go, gs, gx, gz, ga, gt,
     wp, wx, wz, wa, out_b, out_c,
@@ -205,6 +212,8 @@
     chunk_of = []
     for o in (far, up, down, y):
         chunk_of += [(1 - core) * 4 + o, core * 4 + o]
+    w_load = pltpu.make_async_copy(w_ref, w_buf, load_sem.at[8])
+    w_load.start()
     loads = []
     for i, q in enumerate(chunk_of):
         start = pl.multiple_of(q * ch, ch)
@@ -214,11 +223,14 @@
         loads[-1].start()
 
     barrier = pltpu.get_barrier_semaphore()
-    near = [at_u(1), at_u(nu - 1)] + g_peers + snap_peers
+    near = [mate, above, below]
+    near += [(z * NX + lax.rem(x + d, NX), snaps) for d in sorted({1, NX - 1}) if d % NX]
+    near += [(lax.rem(z + d, nz) * NX + x, snaps) for d in sorted({1, nz - 1})]
     for peer in near:
         signal(barrier, peer)
 
-    w_h, w_m, w_l = thirds(w_ref[...])
+    w_load.wait()
+    w_h, w_m, w_l = thirds(w_buf[...])
     w_cat = jnp.concatenate([w_h, w_m, w_l], axis=0)
 
     def sketch_chunk(i):
@@ -230,31 +242,32 @@
     swaps = []
 
     def swap(j):
-        send_a[j] = sketch_chunk(2 * j)
-        if j == 0:
-            pl.semaphore_wait(barrier, len(near))
         swaps.append(remote(send_a.at[j], got_a.at[j], s_a.at[j], r_a.at[j], mate))
         swaps[-1].start()
 
-    known = [1]
-
-    def learn(part):
-        while known[0] < nu // 2:
-            d = known[0]
-            sem = know_sem.at[d.bit_length() - 1]
-            if part == 0:
-                signal(sem, at_u(d))
-                signal(sem, at_u(nu - d))
-                return
-            pl.semaphore_wait(sem, 2)
-            known[0] = 2 * d
-            return
-
+    rounds = [near, near]
+    reach = 1
+    while reach < nu // 2:
+        rounds.append([at_u(reach), at_u(nu - reach)])
+        reach *= 2
+
+    def tell(i):
+        for peer in rounds[i] if i < len(rounds) else ():
+            signal(know_sem.at[i], peer)
+
+    def hear(i):
+        if i < len(rounds):
+            pl.semaphore_wait(know_sem.at[i], len(rounds[i]))
+
+    send_a[0] = sketch_chunk(0)
+    far_part = sketch_chunk(1)
+    send_a[1] = sketch_chunk(2)
+    up_part = sketch_chunk(3)
+    pl.semaphore_wait(barrier, len(near))
     swap(0)
-    learn(0)
-    far_part = sketch_chunk(1)
     swap(1)
-    up_part = sketch_chunk(3)
+    tell(0)
+    send_a[2] = sketch_chunk(4)
     swap(2)
     swaps[0].wait_recv()
     rs_a[...] = far_part + got_a[0]
@@ -262,14 +275,15 @@
     b_up.start()
     b_down = remote(rs_a.at[16:32], rs_b.at[1], s_b.at[1], r_b.at[1], below)
     b_down.start()
-    learn(1)
-    learn(0)
+    hear(0)
+    tell(1)
     down_part = sketch_chunk(5)
     swaps[1].wait_recv()
     up_part = up_part + got_a[1]
     rs_c[0, 16:32] = up_part[16:32]
     c_up = [remote(rs_c.at[0, 16:32], rs_d.at[0, 16:32], s_c.at[0], r_c.at[0], above)]
     c_up[0].start()
+    send_a[3] = sketch_chunk(6)
     swap(3)
     swaps[2].wait_recv()
     down_part = down_part + got_a[2]
@@ -277,6 +291,8 @@
     c_down = [remote(rs_c.at[1, 0:16], rs_d.at[1, 0:16], s_c.at[1], r_c.at[1], below)]
     c_down[0].start()
     own_part = sketch_chunk(7)
+    hear(1)
+    tell(2)
     b_up.wait_recv()
     rs_c[0, 0:16] = up_part[0:16] + rs_b[0]
     c_up.append(remote(rs_c.at[0, 0:16], rs_d.at[0, 0:16], s_c.at[2], r_c.at[2], above))
@@ -287,7 +303,8 @@
     c_down[1].start()
     swaps[3].wait_recv()
     own_part = own_part + got_a[3]
-    learn(1)
+    hear(2)
+    tell(3)
     for copy in c_up + c_down:
         copy.wait_recv()
     own = core * 4 + y
@@ -384,6 +401,15 @@
     passes[2].wait_recv()
     w_sum += projected(2, theirs + up)
     w_sum += projected(1, slot_far)
+
+    hear(3)
+    gx_done = whole(gx, ng - 1, 1)
+    gx_done.wait_recv()
+    hi, lo = pair_sum(gx, ng)
+    gz[u, 0], gz[u, 1] = hi, lo
+    for peer in u_peers:
+        remote(gz.at[u], gz.at[u], s_m.at[3], r_m.at[3], peer).start()
+
     passes[3].wait_recv()
     w_sum += projected(0, theirs + far)
 
@@ -393,13 +419,6 @@
     wx[g] = wp[g]
     for o, peer in zip(g_of, g_peers):
         remote(wp.at[o], wx.at[g], s_m.at[2], r_m.at[2], peer).start()
-
-    gx_done = whole(gx, ng - 1, 1)
-    gx_done.wait_recv()
-    hi, lo = pair_sum(gx, ng)
-    gz[u, 0], gz[u, 1] = hi, lo
-    for peer in u_peers:
-        remote(gz.at[u], gz.at[u], s_m.at[3], r_m.at[3], peer).start()
 
     wx_done = whole(wx, ng - 1, 2)
     wx_done.wait_recv()
@@ -428,13 +447,15 @@
         turned_l = gt[1] if i == 0 else pltpu.roll(gt[1], 128 - n * i, 1)
         tiles_h.append(jnp.where(lane8 < n, turned_h, eye))
         tiles_l.append(jnp.where(lane8 < n, turned_l, 0.0))
-    factor = jnp.concatenate(eliminate(tiles_h, tiles_l), axis=0)
-
     wz_done = whole(wz, nu - 1, 4)
-    wz_done.wait_recv()
-    wa[g] = row_sum(wz, nu)
-    for peer in g_peers:
-        remote(wa.at[g], wa.at[g], s_m.at[6], r_m.at[6], peer).start()
+
+    def share_w():
+        wz_done.wait_recv()
+        wa[g] = row_sum(wz, nu)
+        for peer in g_peers:
+            remote(wa.at[g], wa.at[g], s_m.at[6], r_m.at[6], peer).start()
+
+    factor = jnp.concatenate(eliminate(tiles_h, tiles_l, share_w), axis=0)
 
     f_h, f_m, f_l = thirds(factor)
     f_h, f_m, f_l = f_h.astype(F32), f_m.astype(F32), f_l.astype(F32)
@@ -471,6 +492,28 @@
         copy.wait()
 
 
+def deliver(*arrays):
+    count = len(arrays)
+
+    def body(*refs):
+        copies = [
+            pltpu.make_async_copy(refs[i], refs[count + i], refs[-1].at[i]) for i in range(count)
+        ]
+        for copy in copies:
+            copy.start()
+        for copy in copies:
+            copy.wait()
+
+    return pl.pallas_call(
+        body,
+        out_shape=tuple(jax.ShapeDtypeStruct(a.shape, a.dtype) for a in arrays),
+        in_specs=[pl.BlockSpec(memory_space=pl.ANY)] * count,
+        out_specs=(pl.BlockSpec(memory_space=pl.ANY),) * count,
+        scratch_shapes=[pltpu.SemaphoreType.DMA((count,))],
+        compiler_params=pltpu.CompilerParams(vmem_limit_bytes=1 << 20),
+    )(*arrays)
+
+
 def shards(snapshots, sketch):
     cells, snaps = snapshots.shape
     n = sketch.shape[1]
@@ -480,22 +523,22 @@
     share = n // (2 * NX)
     dma = pltpu.SemaphoreType.DMA
     vm = pltpu.VMEM
-    return pl.pallas_call(
+    basis, coefficients = pl.pallas_call(
         functools.partial(kernel, nz, ch, total),
         out_shape=(
             jax.ShapeDtypeStruct((n, cells), F32),
             jax.ShapeDtypeStruct((n, snaps), F32),
         ),
         in_specs=[
-            pl.BlockSpec(memory_space=pl.ANY),
-            pl.BlockSpec(memory_space=pltpu.VMEM),
+            pl.BlockSpec(memory_space=pltpu.HBM),
+            pl.BlockSpec(memory_space=pltpu.HBM),
         ],
         out_specs=(
             pl.BlockSpec(memory_space=pl.ANY),
             pl.BlockSpec(memory_space=pl.ANY),
         ),
         scratch_shapes=[
-            vm((8, ch, snaps), F32),
+            vm((n, snaps), F32), vm((8, ch, snaps), F32),
             vm((8, ch, snaps), BF16), vm((8, ch, snaps), BF16), vm((8, ch, snaps), BF16),
             vm((4, n, ch), F32), vm((4, n, ch), F32),
             vm((n, ch), F32), vm((2, n // 2, ch), F32),
@@ -507,12 +550,15 @@
             vm((2 * NX, share, snaps), F32), vm((2 * NX, share, snaps), F32),
             vm((nz // 2, share, snaps), F32), vm((2 * NX, share, snaps), F32),
             vm((n, cells), F32), vm((n, snaps), F32),
-            dma((8,)), dma((4,)), dma((4,)), dma((2,)), dma((2,)), dma((4,)), dma((4,)),
+            dma((9,)), dma((4,)), dma((4,)), dma((2,)), dma((2,)), dma((4,)), dma((4,)),
             dma((4,)), dma((4,)), dma((2,)), dma((2,)), dma((4,)), dma((4,)),
-            dma((7,)), dma((7,)), dma((9,)), pltpu.SemaphoreType.REGULAR((2,)),
+            dma((7,)), dma((7,)), dma((9,)), pltpu.SemaphoreType.REGULAR((4,)),
         ],
-        compiler_params=pltpu.CompilerParams(collective_id=0, has_side_effects=True),
+        compiler_params=pltpu.CompilerParams(
+            collective_id=0, has_side_effects=True, vmem_limit_bytes=52 << 20
+        ),
     )(snapshots, jnp.transpose(sketch))
+    return deliver(basis, coefficients)
 
 
 def solution(mesh):

time: 56.4 us -> 52.8 us (0.936)
  local copies, waits for them, and re-layouts: 3.24 us -> 0.75 us
  Pallas kernels: 52.2 us -> 51.2 us
    unnamed x2, local copies, waits for them, and re-layouts: 3.24 us -> 0.75 us
    pallas_call x1, Pallas kernels: 52.2 us -> 50.4 us  [shards(): pl.pallas_call(functools.partial(kernel, nz, ch, total), out_shape=(jax.S...]
    pallas_call x0 -> x1, Pallas kernels: none -> 0.81 us  [deliver(): pl.pallas_call(body, out_shape=tuple((jax.ShapeDtypeStruct(a.shape, a.dty...]
where the time goes in v3:
time: 52.8 us; the launch traced here: 52.6 us
  Pallas kernels  51.2 us (97%)
  local copies, waits for them, and re-layouts  0.75 us (1%)
  between operations  0.65 us (1%)
    pallas_call x1, Pallas kernels, shards(): pl.pallas_call(functools.partial(kernel, nz, ch, total), out_shape=(jax.S...  50.4 us

profile of v3, /device:TPU:1, one launch (start us, length us, event | category | flops | bytes accessed | tf_op | source)
XLA Modules:
  0.0 52.6 jit_solution(9063029223035770879)
XLA Ops:
  0.6 0.0 copy-start
  0.6 0.7 %copy-done = f32[256,32]{0,1:T(8,128)S(1)} copy-done((f32[256,32]{0,1:T(8,128)S(1)}, f32[256,32]{0,1:T(8,128)}, u32[]{:S(2)}) %copy-start) | copy-done | bytes 32792
  1.4 50.4 %shard_map.41 = (f32[32,4096]{1,0:T(8,128)S(1)}, f32[32,256]{1,0:T(8,128)S(1)}) custom-call(f32[4096,256]{1,0:T(8,128)} %a_ref.1, f32[32,256]{1,0:T(8,128)S(1)} %bitcast.1), custom_call_target="tpu_custom_call" | custom-call | tf_op jit(solution)/shard_map/pallas_call | solution.py:526
  51.8 0.8 %shard_map.42 = (f32[32,4096]{1,0:T(8,128)}, f32[32,256]{1,0:T(8,128)}) custom-call(f32[32,4096]{1,0:T(8,128)S(1)} %get-tuple-element.4.refs_0_, f32[32,256]{1,0:T(8,128)S(1)} %get-tuple-element.5.refs_1_), custom_call_target="tpu_custom_call" | custom-call | tf_op jit(solution)/shard_map/pallas_call | solution.py:507
Async XLA Ops:
  0.6 0.8 %copy-start = (f32[256,32]{0,1:T(8,128)S(1)}, f32[256,32]{0,1:T(8,128)}, u32[]{:S(2)}) copy-start(f32[256,32]{0,1:T(8,128)} %param.3) | copy-start | bytes 98308

commit v4 on v3

--- a/solution.py
+++ b/solution.py
@@ -83,9 +83,10 @@
     return p * 2.0, inverse * 0.5
 
 
-def eliminate(gh, gl, midway=None):
+def eliminate(gh, gl, midway=None, block=4):
     gh, gl = list(gh), list(gl)
     tiles = len(gh)
+    last = 8 * tiles - 1
     sub = lax.broadcasted_iota(jnp.int32, (8, 128), 0)
     lane = lax.broadcasted_iota(jnp.int32, (8, 128), 1)
 
@@ -95,31 +96,53 @@
     def down(tile, r):
         return jnp.broadcast_to(tile[r : r + 1, :], (8, 128))
 
-    for k in range(8 * tiles - 1):
-        if midway is not None and k == 24:
+    for start in range(0, last, block):
+        if midway is not None and start == 16:
             midway()
-        ib, kr = divmod(k, 8)
-        columns = {t: (across(gh[t], k), across(gl[t], k)) for t in range(ib, tiles)}
-        ph, plo = down(columns[ib][0], kr), down(columns[ib][1], kr)
-        rh, rl = down(gh[ib], kr), down(gl[ib], kr)
-        r = 1.0 / ph
-        pa, pb = halves(ph)
-        q1 = rh * r
-        qa, qb = halves(q1)
-        t, te = two_prod(q1, qa, qb, ph, pa, pb)
-        rest = (rh - t) - te + (rl - q1 * plo)
-        uh, ul = quick_two_sum(q1, rest * r)
-        ua, ub = halves(uh)
-        for t in range(ib if kr < 7 else ib + 1, tiles):
-            ch, cl = columns[t]
-            if t == ib:
-                ch = jnp.where(sub > kr, ch, 0.0)
-                cl = jnp.where(sub > kr, cl, 0.0)
-            ca, cb = halves(ch)
-            p, pe = two_prod(ch, ca, cb, uh, ua, ub)
-            pe = pe + (ch * ul + cl * uh)
-            s, e = two_sum(gh[t], -p)
-            gh[t], gl[t] = quick_two_sum(s, e + (gl[t] - pe))
+        ib = start // 8
+        columns = [
+            {t: (across(gh[t], k), across(gl[t], k)) for t in range(ib, tiles)}
+            for k in range(start, start + block)
+        ]
+        for j in range(block):
+            k, kr = start + j, (start + j) % 8
+            if k == last:
+                break
+            ph, plo = (down(v, kr) for v in columns[j][ib])
+            r = 1.0 / ph
+            ra, rb = halves(r)
+
+            def scaled(h, low):
+                ha, hb = halves(h)
+                p, e = two_prod(h, ha, hb, r, ra, rb)
+                return p, e + low * r
+
+            one, rest = scaled(ph, plo)
+            slip = (one - 1.0) + rest
+            uh, ul = scaled(down(gh[ib], kr), down(gl[ib], kr))
+            rows = [(uh, ul) + halves(uh)]
+            for i in range(j + 1, block):
+                vh, vl = scaled(*(down(v, kr) for v in columns[i][ib]))
+                rows.append((vh, vl) + halves(vh))
+            for t in range(ib if kr < 7 else ib + 1, tiles):
+                ch, cl = columns[j][t]
+                slip_t = slip
+                if t == ib:
+                    ch = jnp.where(sub > kr, ch, 0.0)
+                    cl = jnp.where(sub > kr, cl, 0.0)
+                    slip_t = jnp.where(sub > kr, slip, 0.0)
+                ca, cb = halves(ch)
+
+                def reduced(h, low, row):
+                    vh, vl, va, vb = row
+                    p, e = two_prod(ch, ca, cb, vh, va, vb)
+                    e = (ch * vl + cl * vh) + e
+                    s, d = two_sum(h, -p)
+                    return quick_two_sum(s, d + ((low + h * slip_t) - e))
+
+                gh[t], gl[t] = reduced(gh[t], gl[t], rows[0])
+                for i in range(j + 1, block):
+                    columns[i][t] = reduced(*columns[i][t], rows[i - j])
     out = []
     for t in range(tiles):
         at = lane == sub + 8 * t
@@ -260,21 +283,21 @@
             pl.semaphore_wait(know_sem.at[i], len(rounds[i]))
 
     send_a[0] = sketch_chunk(0)
+    pl.semaphore_wait(barrier, len(near))
+    swap(0)
     far_part = sketch_chunk(1)
     send_a[1] = sketch_chunk(2)
-    up_part = sketch_chunk(3)
-    pl.semaphore_wait(barrier, len(near))
-    swap(0)
     swap(1)
     tell(0)
-    send_a[2] = sketch_chunk(4)
-    swap(2)
     swaps[0].wait_recv()
     rs_a[...] = far_part + got_a[0]
     b_up = remote(rs_a.at[0:16], rs_b.at[0], s_b.at[0], r_b.at[0], above)
     b_up.start()
     b_down = remote(rs_a.at[16:32], rs_b.at[1], s_b.at[1], r_b.at[1], below)
     b_down.start()
+    up_part = sketch_chunk(3)
+    send_a[2] = sketch_chunk(4)
+    swap(2)
     hear(0)
     tell(1)
     down_part = sketch_chunk(5)

time: 52.8 us -> 48.8 us (0.924)
  Pallas kernels: 51.2 us -> 47.3 us
    pallas_call x1, Pallas kernels: 50.4 us -> 46.5 us  [shards(): pl.pallas_call(functools.partial(kernel, nz, ch, total), out_shape=(jax.S...]
where the time goes in v4:
time: 48.8 us; the launch traced here: 48.7 us
  Pallas kernels  47.3 us (97%)
  local copies, waits for them, and re-layouts  0.75 us (2%)
  between operations  0.65 us (1%)
    pallas_call x1, Pallas kernels, shards(): pl.pallas_call(functools.partial(kernel, nz, ch, total), out_shape=(jax.S...  46.5 us

profile of v4, /device:TPU:1, one launch (start us, length us, event | category | flops | bytes accessed | tf_op | source)
XLA Modules:
  0.0 48.7 jit_solution(5128070759383905569)
XLA Ops:
  0.6 0.0 copy-start
  0.6 0.7 %copy-done = f32[256,32]{0,1:T(8,128)S(1)} copy-done((f32[256,32]{0,1:T(8,128)S(1)}, f32[256,32]{0,1:T(8,128)}, u32[]{:S(2)}) %copy-start) | copy-done | bytes 32792
  1.4 46.5 %shard_map.41 = (f32[32,4096]{1,0:T(8,128)S(1)}, f32[32,256]{1,0:T(8,128)S(1)}) custom-call(f32[4096,256]{1,0:T(8,128)} %a_ref.1, f32[32,256]{1,0:T(8,128)S(1)} %bitcast.1), custom_call_target="tpu_custom_call" | custom-call | tf_op jit(solution)/shard_map/pallas_call | solution.py:549
  47.8 0.8 %shard_map.42 = (f32[32,4096]{1,0:T(8,128)}, f32[32,256]{1,0:T(8,128)}) custom-call(f32[32,4096]{1,0:T(8,128)S(1)} %get-tuple-element.4.refs_0_, f32[32,256]{1,0:T(8,128)S(1)} %get-tuple-element.5.refs_1_), custom_call_target="tpu_custom_call" | custom-call | tf_op jit(solution)/shard_map/pallas_call | solution.py:530
Async XLA Ops:
  0.6 0.8 %copy-start = (f32[256,32]{0,1:T(8,128)S(1)}, f32[256,32]{0,1:T(8,128)}, u32[]{:S(2)}) copy-start(f32[256,32]{0,1:T(8,128)} %param.3) | copy-start | bytes 98308

commit v5 on v4

--- a/solution.py
+++ b/solution.py
@@ -213,9 +213,11 @@
     mate = (cells, 2 * y + 1 - core)
     above = (cells, 2 * up + core)
     below = (cells, 2 * down + core)
+    above_mate = (cells, 2 * up + 1 - core)
+    below_mate = (cells, 2 * down + 1 - core)
     snap_of = [lax.rem(snaps + d, 8) for d in (4, 5, 3, 2, 6, 1, 7)]
     snap_peers = [(cells, s) for s in snap_of]
-    g_of = [lax.rem(g + d, ng) for d in range(1, ng)]
+    g_of = [lax.rem(g + d, ng) for d in sorted(range(1, ng), key=lambda d: -min(d, ng - d))]
     g_peers = [((2 * u + lax.rem(o, 2)) * NX + lax.div(o, 2), snaps) for o in g_of]
 
     def at_u(d):
@@ -243,7 +245,9 @@
         loads.append(
             pltpu.make_async_copy(a_ref.at[pl.ds(start, ch), :], a_buf.at[i], load_sem.at[i])
         )
-        loads[-1].start()
+    ahead = 2
+    for load in loads[:ahead]:
+        load.start()
 
     barrier = pltpu.get_barrier_semaphore()
     near = [mate, above, below]
@@ -258,6 +262,8 @@
 
     def sketch_chunk(i):
         loads[i].wait()
+        for load in loads[ahead + 2 * i : ahead + 2 * i + 2]:
+            load.start()
         h, m, low = thirds(a_buf[i])
         a_h[i], a_m[i], a_l[i] = h, m, low
         return six(w_cat, h, m, low, True)
@@ -363,16 +369,23 @@
     for r in range(8):
         go[r, 0] = gram_h[r : r + 1]
         go[r, 1] = gram_l[r : r + 1]
-    gs[snaps] = go[snaps]
+
+    def quarter_of(s):
+        return 2 * lax.rem(s, 2) + lax.rem(lax.div(s, 2), 2)
+
+    quarter = quarter_of(snaps)
+    for r in range(2):
+        gs[snaps, r] = go[2 * quarter + r]
     for s, peer in zip(snap_of, snap_peers):
-        remote(go.at[s], gs.at[snaps], s_m.at[0], r_m.at[0], peer).start()
+        piece = go.at[pl.ds(2 * quarter_of(s), 2)]
+        remote(piece, gs.at[snaps], s_m.at[0], r_m.at[0], peer).start()
 
     def whole(buf, count, sem):
         piece = buf.at[pl.ds(0, count)]
         return remote(piece, piece, s_m.at[sem], r_m.at[sem], mate)
 
     def pair_sum(buf, count):
-        return sum_pairs([(buf[i, 0], buf[i, 1]) for i in range(count)])
+        return sum_pairs([(buf[i, :, 0], buf[i, :, 1]) for i in range(count)])
 
     def row_sum(buf, count):
         rows = [buf[i] for i in range(count)]
@@ -397,11 +410,15 @@
     passes[0].wait_recv()
     w_sum += projected(6, theirs + y)
     along(slot_down, first, 0, above, s_y, r_y).wait_recv()
-    f_up = along(slot_down, first, 0, above, s_f, r_f)
-    f_up.start()
+    forwards = [along(slot_down, first, 0, above, s_f, r_f)]
+    forwards[0].start()
     along(slot_up, second, 1, below, s_y, r_y).wait_recv()
-    f_down = along(slot_up, second, 1, below, s_f, r_f)
-    f_down.start()
+    forwards.append(along(slot_up, second, 1, below, s_f, r_f))
+    forwards[1].start()
+    forwards.append(along(slot_down, first, 2, above_mate, s_f, r_f))
+    forwards[2].start()
+    forwards.append(along(slot_up, second, 3, below_mate, s_f, r_f))
+    forwards[3].start()
     along(slot_down, second, 2, above, s_y, r_y).wait_recv()
     pass_on(slot_down)
     along(slot_up, first, 3, below, s_y, r_y).wait_recv()
@@ -410,15 +427,14 @@
     gs_done = whole(gs, 7, 0)
     gs_done.wait_recv()
     hi, lo = pair_sum(gs, 8)
-    gx[g, 0], gx[g, 1] = hi, lo
+    gx[g, :, 0], gx[g, :, 1] = hi, lo
     for peer in g_peers:
         remote(gx.at[g], gx.at[g], s_m.at[1], r_m.at[1], peer).start()
 
     w_sum += projected(5, slot_down)
     w_sum += projected(3, slot_up)
-    f_up.wait_recv()
-    f_down.wait_recv()
-    pass_on(slot_far)
+    forwards[0].wait_recv()
+    forwards[1].wait_recv()
     passes[1].wait_recv()
     w_sum += projected(4, theirs + down)
     passes[2].wait_recv()
@@ -429,11 +445,12 @@
     gx_done = whole(gx, ng - 1, 1)
     gx_done.wait_recv()
     hi, lo = pair_sum(gx, ng)
-    gz[u, 0], gz[u, 1] = hi, lo
+    gz[u, :, 0], gz[u, :, 1] = hi, lo
     for peer in u_peers:
         remote(gz.at[u], gz.at[u], s_m.at[3], r_m.at[3], peer).start()
 
-    passes[3].wait_recv()
+    forwards[2].wait_recv()
+    forwards[3].wait_recv()
     w_sum += projected(0, theirs + far)
 
     share = n // ng
@@ -452,15 +469,16 @@
     gz_done = whole(gz, nu - 1, 3)
     gz_done.wait_recv()
     hi, lo = pair_sum(gz, nu)
-    ga[snaps, 0], ga[snaps, 1] = hi, lo
-    for peer in snap_peers:
-        remote(ga.at[snaps], ga.at[snaps], s_m.at[5], r_m.at[5], peer).start()
-    ga_done = whole(ga, 7, 5)
+    ga[quarter, :, 0], ga[quarter, :, 1] = hi, lo
+    twin = 4 * lax.div(y, 2) + 2 - 2 * lax.rem(y, 2)
+    for peer in ((cells, twin + core), (cells, twin + 1 - core), mate):
+        remote(ga.at[quarter], ga.at[quarter], s_m.at[5], r_m.at[5], peer).start()
+    ga_done = whole(ga, 3, 5)
     ga_done.wait_recv()
 
     for r in range(8):
-        gt[0, r : r + 1, :] = ga[r, 0]
-        gt[1, r : r + 1, :] = ga[r, 1]
+        gt[0, r : r + 1, :] = ga[r // 2, r % 2, 0]
+        gt[1, r : r + 1, :] = ga[r // 2, r % 2, 1]
     lane8 = lax.broadcasted_iota(jnp.int32, (8, 128), 1)
     sub8 = lax.broadcasted_iota(jnp.int32, (8, 128), 0)
     tiles_h, tiles_l = [], []
@@ -507,7 +525,7 @@
     writes.append(pltpu.make_async_copy(out_c, coef_ref, out_sem.at[8]))
     writes[-1].start()
 
-    for copy in swaps + [b_up, b_down] + c_up + c_down + gathers + [f_up, f_down] + passes:
+    for copy in swaps + [b_up, b_down] + c_up + c_down + gathers + forwards + passes:
         copy.wait_send()
     for copy in (gs_done, gx_done, wx_done, gz_done, wz_done, ga_done, wa_done):
         copy.wait_send()
@@ -517,11 +535,17 @@
 
 def deliver(*arrays):
     count = len(arrays)
+    pieces = [(i, r) for i, a in enumerate(arrays) for r in range(0, a.shape[0], 8)]
 
     def body(*refs):
-        copies = [
-            pltpu.make_async_copy(refs[i], refs[count + i], refs[-1].at[i]) for i in range(count)
-        ]
+        copies = []
+        for sem, (i, r) in enumerate(pieces):
+            rows = pl.ds(r, 8)
+            copies.append(
+                pltpu.make_async_copy(
+                    refs[i].at[rows, :], refs[count + i].at[rows, :], refs[-1].at[sem]
+                )
+            )
         for copy in copies:
             copy.start()
         for copy in copies:
@@ -532,7 +556,7 @@
         out_shape=tuple(jax.ShapeDtypeStruct(a.shape, a.dtype) for a in arrays),
         in_specs=[pl.BlockSpec(memory_space=pl.ANY)] * count,
         out_specs=(pl.BlockSpec(memory_space=pl.ANY),) * count,
-        scratch_shapes=[pltpu.SemaphoreType.DMA((count,))],
+        scratch_shapes=[pltpu.SemaphoreType.DMA((len(pieces),))],
         compiler_params=pltpu.CompilerParams(vmem_limit_bytes=1 << 20),
     )(*arrays)
 
@@ -567,14 +591,14 @@
             vm((n, ch), F32), vm((2, n // 2, ch), F32),
             vm((2, n, ch), F32), vm((2, n, ch), F32),
             vm((8, n, ch), F32), vm((8, 6 * n, ch), BF16),
-            vm((8, 2, 1, 128), F32), vm((8, 2, 1, 128), F32),
-            vm((2 * NX, 2, 1, 128), F32), vm((nz // 2, 2, 1, 128), F32),
-            vm((8, 2, 1, 128), F32), vm((2, 8, 128), F32),
+            vm((8, 2, 1, 128), F32), vm((8, 2, 2, 1, 128), F32),
+            vm((2 * NX, 2, 2, 1, 128), F32), vm((nz // 2, 2, 2, 1, 128), F32),
+            vm((4, 2, 2, 1, 128), F32), vm((2, 8, 128), F32),
             vm((2 * NX, share, snaps), F32), vm((2 * NX, share, snaps), F32),
             vm((nz // 2, share, snaps), F32), vm((2 * NX, share, snaps), F32),
             vm((n, cells), F32), vm((n, snaps), F32),
             dma((9,)), dma((4,)), dma((4,)), dma((2,)), dma((2,)), dma((4,)), dma((4,)),
-            dma((4,)), dma((4,)), dma((2,)), dma((2,)), dma((4,)), dma((4,)),
+            dma((4,)), dma((4,)), dma((4,)), dma((4,)), dma((3,)), dma((3,)),
             dma((7,)), dma((7,)), dma((9,)), pltpu.SemaphoreType.REGULAR((4,)),
         ],
         compiler_params=pltpu.CompilerParams(

time: 48.8 us -> 48.4 us (level)
  Pallas kernels: 47.3 us -> 46.8 us
    pallas_call x1, Pallas kernels: 46.5 us -> 45.9 us  [shards(): pl.pallas_call(functools.partial(kernel, nz, ch, total), out_shape=(jax.S...]
where the time goes in v5:
time: 48.4 us; the launch traced here: 48.2 us
  Pallas kernels  46.8 us (97%)
  local copies, waits for them, and re-layouts  0.75 us (2%)
  between operations  0.65 us (1%)
    pallas_call x1, Pallas kernels, shards(): pl.pallas_call(functools.partial(kernel, nz, ch, total), out_shape=(jax.S...  45.9 us

profile of v5, /device:TPU:1, one launch (start us, length us, event | category | flops | bytes accessed | tf_op | source)
XLA Modules:
  0.0 48.2 jit_solution(17828440467685296503)
XLA Ops:
  0.6 0.0 copy-start
  0.6 0.7 %copy-done = f32[256,32]{0,1:T(8,128)S(1)} copy-done((f32[256,32]{0,1:T(8,128)S(1)}, f32[256,32]{0,1:T(8,128)}, u32[]{:S(2)}) %copy-start) | copy-done | bytes 32792
  1.4 45.9 %shard_map.41 = (f32[32,4096]{1,0:T(8,128)S(1)}, f32[32,256]{1,0:T(8,128)S(1)}) custom-call(f32[4096,256]{1,0:T(8,128)} %a_ref.1, f32[32,256]{1,0:T(8,128)S(1)} %bitcast.1), custom_call_target="tpu_custom_call" | custom-call | tf_op jit(solution)/shard_map/pallas_call | solution.py:573
  47.3 0.9 %shard_map.42 = (f32[32,4096]{1,0:T(8,128)}, f32[32,256]{1,0:T(8,128)}) custom-call(f32[32,4096]{1,0:T(8,128)S(1)} %get-tuple-element.4.refs_0_, f32[32,256]{1,0:T(8,128)S(1)} %get-tuple-element.5.refs_1_), custom_call_target="tpu_custom_call" | custom-call | tf_op jit(solution)/shard_map/pallas_call | solution.py:554
Async XLA Ops:
  0.6 0.8 %copy-start = (f32[256,32]{0,1:T(8,128)S(1)}, f32[256,32]{0,1:T(8,128)}, u32[]{:S(2)}) copy-start(f32[256,32]{0,1:T(8,128)} %param.3) | copy-start | bytes 98308

commit v6 on v5

--- a/solution.py
+++ b/solution.py
@@ -517,6 +517,13 @@
         )
         writes[-1].start()
 
+    for copy in swaps + [b_up, b_down] + c_up + c_down + gathers + forwards + passes:
+        copy.wait_send()
+    for copy in (gs_done, gx_done, wx_done, gz_done, wz_done, ga_done):
+        copy.wait_send()
+    for copy in writes:
+        copy.wait()
+
     wa_done = whole(wa, ng - 1, 6)
     wa_done.wait_recv()
     w_total = jnp.concatenate([wa[i] for i in range(ng)], axis=0)
@@ -525,12 +532,8 @@
     writes.append(pltpu.make_async_copy(out_c, coef_ref, out_sem.at[8]))
     writes[-1].start()
 
-    for copy in swaps + [b_up, b_down] + c_up + c_down + gathers + forwards + passes:
-        copy.wait_send()
-    for copy in (gs_done, gx_done, wx_done, gz_done, wz_done, ga_done, wa_done):
-        copy.wait_send()
-    for copy in writes:
-        copy.wait()
+    writes[-1].wait()
+    wa_done.wait_send()
 
 
 def deliver(*arrays):

time: 48.4 us -> 48.3 us (level)
  no operation moved by 1% of the time
where the time goes in v6:
time: 48.3 us; the launch traced here: 48.1 us
  Pallas kernels  46.7 us (97%)
  local copies, waits for them, and re-layouts  0.75 us (2%)
  between operations  0.65 us (1%)
    pallas_call x1, Pallas kernels, shards(): pl.pallas_call(functools.partial(kernel, nz, ch, total), out_shape=(jax.S...  45.9 us

profile of v6, /device:TPU:1, one launch (start us, length us, event | category | flops | bytes accessed | tf_op | source)
XLA Modules:
  0.0 48.1 jit_solution(2330160636592363147)
XLA Ops:
  0.6 0.0 copy-start
  0.6 0.7 %copy-done = f32[256,32]{0,1:T(8,128)S(1)} copy-done((f32[256,32]{0,1:T(8,128)S(1)}, f32[256,32]{0,1:T(8,128)}, u32[]{:S(2)}) %copy-start) | copy-done | bytes 32792
  1.4 45.9 %shard_map.41 = (f32[32,4096]{1,0:T(8,128)S(1)}, f32[32,256]{1,0:T(8,128)S(1)}) custom-call(f32[4096,256]{1,0:T(8,128)} %a_ref.1, f32[32,256]{1,0:T(8,128)S(1)} %bitcast.1), custom_call_target="tpu_custom_call" | custom-call | tf_op jit(solution)/shard_map/pallas_call | solution.py:576
  47.3 0.9 %shard_map.42 = (f32[32,4096]{1,0:T(8,128)}, f32[32,256]{1,0:T(8,128)}) custom-call(f32[32,4096]{1,0:T(8,128)S(1)} %get-tuple-element.4.refs_0_, f32[32,256]{1,0:T(8,128)S(1)} %get-tuple-element.5.refs_1_), custom_call_target="tpu_custom_call" | custom-call | tf_op jit(solution)/shard_map/pallas_call | solution.py:557
Async XLA Ops:
  0.6 0.8 %copy-start = (f32[256,32]{0,1:T(8,128)S(1)}, f32[256,32]{0,1:T(8,128)}, u32[]{:S(2)}) copy-start(f32[256,32]{0,1:T(8,128)} %param.3) | copy-start | bytes 98308
